TPU v7x, 128 devices: a whole 4x4x4 slice. The times are simulated.
128 devices in a mesh: dp: 8 (over z, core), mp: 16 (over y, x).
Axes of the slice: x: 4, y: 4, z: 4, core: 2. Of those that a mesh axis runs over, the one named last changes fastest.
Arguments:
- stream: bfloat16 [65536, 2048], P(('dp', 'mp')), may hold values from -5.5 to 5.5
- norm_weight: float32 [2048], replicated, may hold values from 0.5 to 1.5
- query_key_weight: bfloat16 [2048, 512], P(('dp', 'mp')), may hold values from -0.25 to 0.25
- value_weight: bfloat16 [2048, 2048], P(('dp', 'mp')), may hold values from -0.125 to 0.125
- output_weight: bfloat16 [2048, 2048], P(('dp', 'mp')), may hold values from -0.5 to 0.5
- convolution_weights: float32 [3, 2048], replicated, may hold values from -2.5 to 2.5
- adapter_down_maps: bfloat16 [64, 16, 2048], P('mp'), may hold values from -0.125 to 0.125
- adapter_up_maps: bfloat16 [64, 16, 2048], P('mp'), may hold values from -1.5 to 1.5
- prompt_lengths: int32 [128, 8], P(('dp', 'mp')), may hold values from 1 to 256, 512 in all within a row
- block_adapter_index: int32 [2048], P(('dp', 'mp')), may hold values from 0 to 63, as said below
Outputs:
- hidden: bfloat16 [65536, 2048], P(('dp', 'mp'))
Inputs may be any that keep to these rules, and one draw needn't show every extreme that they name: `prompt_lengths`: each row holds the lengths of one device's 8 prompts; a row sums to 512 and its largest entry is exactly 256. `block_adapter_index`: adapters k * 4 to (k + 1) * 4 - 1 sit on index k of mp. The 16 blocks of one device name adapters of any one index of mp at most 2 times; in every draw, on each index of dp, one index of mp is named exactly 2 times by every device.
All inputs are finite; a program needn't handle non-finite values.
Results may differ from a plain program's by a relative error of at most 0.0088.
Values may be sent and summed in bfloat16 or wider, within the bound.
A program may use at most 128 MiB of HBM per device.

v0:
```python
import math
import jax
import jax.numpy as jnp
from jax import lax
from jax.sharding import PartitionSpec as P

HEADS = 16
QK = 16
adapter_scale = 2.0
norm_eps = 1e-05


def prompt_index(lengths, total_token_count):
    bounds = jnp.cumsum(lengths)
    position = jnp.arange(total_token_count, dtype=jnp.int32)
    return jnp.sum((position[:, None] >= bounds[None, :]).astype(jnp.int32), axis=1)


def short_conv(value_matrix, tap_table, segment):
    result = tap_table[0][None, :] * value_matrix
    for offset in range(1, tap_table.shape[0]):
        earlier = jnp.concatenate(
            [jnp.zeros((offset, value_matrix.shape[1]), jnp.float32), value_matrix[:-offset]],
            axis=0,
        )
        same_prompt = jnp.concatenate(
            [jnp.zeros((offset,), jnp.bool_), segment[offset:] == segment[:-offset]], axis=0
        )
        result = result + tap_table[offset][None, :] * jnp.where(same_prompt[:, None], earlier, 0.0)
    return result


def taylor_heads(query_key, mixed, segment, head_count, feature):
    total_token_count, hidden_width = mixed.shape
    head_width = hidden_width // head_count
    queries = (
        query_key[:, : head_count * feature]
        .reshape(total_token_count, head_count, feature)
        .transpose(1, 0, 2)
    )
    key_rows = (
        query_key[:, head_count * feature :]
        .reshape(total_token_count, head_count, feature)
        .transpose(1, 0, 2)
    )
    value_rows = mixed.reshape(total_token_count, head_count, head_width).transpose(1, 0, 2)
    position = jnp.arange(total_token_count, dtype=jnp.int32)
    allowed = (position[None, :] <= position[:, None]) & (segment[None, :] == segment[:, None])
    score_scale = 1.0 / math.sqrt(feature)

    def one_head(operands):
        query_one, key_one, value_one = operands
        scores = jnp.dot(query_one, key_one.T, preferred_element_type=jnp.float32) * score_scale
        weight = jnp.where(allowed, 1.0 + scores + 0.5 * scores * scores, 0.0)
        row_total = jnp.sum(weight, axis=1, keepdims=True)
        numerator = jnp.dot(
            weight.astype(jnp.bfloat16), value_one, preferred_element_type=jnp.float32
        )
        return numerator / row_total

    outputs = lax.map(one_head, (queries, key_rows, value_rows))
    return outputs.transpose(1, 0, 2).reshape(total_token_count, hidden_width).astype(jnp.bfloat16)


def local(
    stream,
    norm_weight,
    query_key_weight,
    value_weight,
    output_weight,
    convolution_weights,
    adapter_down_maps,
    adapter_up_maps,
    prompt_lengths,
    block_adapter_index,
):
    total_token_count, hidden_width = stream.shape
    stream_f = stream.astype(jnp.float32)
    mean_sq = jnp.mean(stream_f * stream_f, axis=1, keepdims=True)
    normed = (stream_f * lax.rsqrt(mean_sq + norm_eps) * norm_weight[None, :]).astype(jnp.bfloat16)
    inputs = normed
    qk_sum = jnp.dot(
        inputs,
        lax.all_gather(query_key_weight, ("dp", "mp"), axis=0, tiled=True),
        preferred_element_type=jnp.float32,
    )
    plain_value_rows = jnp.dot(
        inputs,
        lax.all_gather(value_weight, ("dp", "mp"), axis=0, tiled=True),
        preferred_element_type=jnp.float32,
    )
    query_key = qk_sum.astype(jnp.bfloat16)
    holders = lax.axis_size("mp")
    local_token_count = adapter_down_maps.shape[0]
    adapter_width = adapter_down_maps.shape[1]
    block_count = block_adapter_index.shape[0]
    block_rows = total_token_count // block_count
    capacity = 2 * block_count // holders
    holder_of = block_adapter_index // local_token_count
    within = (block_adapter_index % local_token_count).astype(jnp.float32)
    onehot = (holder_of[:, None] == jnp.arange(holders, dtype=jnp.int32)[None, :]).astype(jnp.int32)
    slot_index = jnp.sum((jnp.cumsum(onehot, axis=0) - 1) * onehot, axis=1)
    target = holder_of * capacity + slot_index
    select = (jnp.arange(holders * capacity, dtype=jnp.int32)[:, None] == target[None, :]).astype(
        jnp.bfloat16
    )
    outgoing = jnp.dot(
        select,
        normed.reshape(block_count, block_rows * hidden_width),
        preferred_element_type=jnp.float32,
    )
    outgoing = outgoing.astype(jnp.bfloat16).reshape(holders, capacity * block_rows, hidden_width)
    slot_local = jnp.dot(select.astype(jnp.float32), within, preferred_element_type=jnp.float32)
    slot_local = (
        jnp.repeat(slot_local, block_rows)
        .astype(jnp.bfloat16)
        .reshape(holders, capacity * block_rows)
    )
    flattened_down = adapter_down_maps.reshape(local_token_count * adapter_width, hidden_width)
    flattened_up = adapter_up_maps.reshape(local_token_count * adapter_width, hidden_width)
    column_owner = (
        jnp.arange(local_token_count * adapter_width, dtype=jnp.int32) // adapter_width
    ).astype(jnp.float32)
    rows_here = lax.all_to_all(outgoing, "mp", split_axis=0, concat_axis=0, tiled=True)
    local_ids = lax.all_to_all(slot_local, "mp", split_axis=0, concat_axis=0, tiled=True)
    low_all = jnp.einsum(
        "skd,cd->skc", rows_here, flattened_down, preferred_element_type=jnp.float32
    )
    keep = local_ids.astype(jnp.float32)[:, :, None] == column_owner[None, None, :]
    reduced_rows = jnp.where(keep, low_all, 0.0).astype(jnp.bfloat16)
    value_update = adapter_scale * jnp.einsum(
        "skc,cd->skd", reduced_rows, flattened_up, preferred_element_type=jnp.float32
    )
    returned = lax.all_to_all(
        value_update.astype(jnp.bfloat16), "mp", split_axis=0, concat_axis=0, tiled=True
    )
    adapter_delta = jnp.dot(
        select.T,
        returned.reshape(holders * capacity, block_rows * hidden_width),
        preferred_element_type=jnp.float32,
    )
    adapter_delta = adapter_delta.reshape(total_token_count, hidden_width)
    value_matrix = plain_value_rows + adapter_delta
    segment = prompt_index(prompt_lengths[0], total_token_count)
    conv = short_conv(value_matrix, convolution_weights, segment)
    mixed = (conv * jax.nn.silu(value_matrix)).astype(jnp.bfloat16)
    attended = taylor_heads(query_key, mixed, segment, HEADS, QK)
    inputs = attended
    projected = jnp.dot(
        inputs,
        lax.all_gather(output_weight, ("dp", "mp"), axis=0, tiled=True),
        preferred_element_type=jnp.float32,
    )
    return (stream_f + projected).astype(jnp.bfloat16)


def solution(mesh):
    return jax.shard_map(
        local,
        mesh=mesh,
        in_specs=(
            P(("dp", "mp"), None),
            P(),
            P(("dp", "mp"), None),
            P(("dp", "mp"), None),
            P(("dp", "mp"), None),
            P(),
            P("mp", None, None),
            P("mp", None, None),
            P(("dp", "mp"), None),
            P(("dp", "mp")),
        ),
        out_specs=P(("dp", "mp"), None),
        check_vma=False,
    )
```

profile of v0, /device:TPU:1, one launch (start us, length us, event | category | flops | bytes accessed | tf_op | source)
XLA Modules:
  0.0 303.8 jit_solution(3091795847900209915)
XLA Ops:
  6.5 0.7 all-gather.4.cloned.1.call-update
  7.3 0.7 all-gather.6.cloned.1.call-update
  8.0 0.7 and_select_fusion.2
  9.0 0.7 multiply_add_fusion
  9.6 0.8 fusion.19
  10.6 0.7 convert_element_type.107
  11.3 7.6 %all-to-all-start = ((bf16[16,1,64]{2,1,0:T(2,128)(2,1)}), bf16[16,1,64]{2,1,0:T(2,128)(2,1)S(1)}, u32[]{:S(2)}, u32[]{:S(2)}) async-start(bf16[16,1,64]{2,1,0:T(2,128)(2,1)} %convert_element_type.107), calls=%async_computation | async-start | bytes 16384 | tf_op jit(solution)/shard_map/all_to_all | solution.py:125
  18.9 2.1 fusion.13
  21.0 3.5 %fusion.15 = bf16[512,2048]{1,0:T(8,128)(2,1)} fusion(bf16[512,2048]{1,0:T(8,128)(2,1)} %param.12, f32[2048]{0:T(1024)} %param.13, f32[512]{0:T(512)S(1)} %add_rsqrt_fusion), kind=kLoop, calls=%fused_computation.23 | loop fusion | flops 4194304 | bytes 4204544 | tf_op jit(solution)/shard_map/convert_element_type | solution.py:80
  24.4 2.2 reshape.118
  26.6 3.2 %convolution_convert_fusion = bf16[32,65536]{1,0:T(8,128)(2,1)} fusion(bf16[16,65536]{1,0:T(8,128)(2,1)S(1)} %reshape.118, s32[16]{0:T(128)S(1)} %multiply_add_fusion), kind=kOutput, calls=%fused_computation.16 | convolution fusion | flops 69206528 | bytes 6291520 | tf_op jit(solution)/shard_map/dot_general | solution.py:107
  29.8 5.6 %reshape.119 = bf16[16,64,2048]{2,1,0:T(8,128)(2,1)} reshape(bf16[32,65536]{1,0:T(8,128)(2,1)} %convolution_convert_fusion) | data formatting | bytes 8388608 | tf_op jit(solution)/shard_map/reshape | solution.py:112
  35.5 6.8 %all-to-all-start.1 = ((bf16[16,64,2048]{2,1,0:T(8,128)(2,1)}), bf16[16,64,2048]{2,1,0:T(8,128)(2,1)}, u32[]{:S(2)}, u32[]{:S(2)}) async-start(bf16[16,64,2048]{2,1,0:T(8,128)(2,1)} %reshape.119), calls=%async_computation.1 | async-start | bytes 8388608 | tf_op jit(solution)/shard_map/all_to_all | solution.py:124
  42.3 0.7 all-gather.8.cloned.1.call-update
  43.1 61.8 %all-to-all-done.1 = bf16[16,64,2048]{2,1,0:T(8,128)(2,1)} async-done(((bf16[16,64,2048]{2,1,0:T(8,128)(2,1)}), bf16[16,64,2048]{2,1,0:T(8,128)(2,1)}, u32[]{:S(2)}, u32[]{:S(2)}) %all-to-all-start.1) | async-done | bytes 4194336 | tf_op jit(solution)/shard_map/all_to_all | solution.py:124
  104.8 8.5 %multiply_convert_fusion = bf16[16,64,2048]{2,1,0:T(8,128)(2,1)} fusion(bf16[64,2048,1]{1,0,2:T(8,128)(2,1)S(1)} %bitcast.74, bf16[16,64,2048]{2,1,0:T(8,128)(2,1)} %all-to-all-done.1, bf16[64,2048,1]{1,0,2:T(8,128)(2,1)S(1)} %bitcast.79, f32[64]{0:T(128)S(1)} %fusion.29, f32[16,64]{1,0:T(8,128)S(1)} %bitcast.83), kind=kOutput, calls=%fused_computation.17 | convolution fusion | flops 541261824 | bytes 8917248 | tf_op jit(solution)/shard_map/skc,cd->skd/dot_general | solution.py:131
  113.4 4.9 %all-to-all-start.2 = ((bf16[16,64,2048]{2,1,0:T(8,128)(2,1)}), bf16[16,64,2048]{2,1,0:T(8,128)(2,1)}, u32[]{:S(2)}, u32[]{:S(2)}) async-start(bf16[16,64,2048]{2,1,0:T(8,128)(2,1)} %multiply_convert_fusion), calls=%async_computation.2 | async-start | bytes 8388608 | tf_op jit(solution)/shard_map/all_to_all | solution.py:134
  118.9 2.9 convolution_convert_fusion.1
  121.9 53.5 %all-to-all-done.2 = bf16[16,64,2048]{2,1,0:T(8,128)(2,1)} async-done(((bf16[16,64,2048]{2,1,0:T(8,128)(2,1)}), bf16[16,64,2048]{2,1,0:T(8,128)(2,1)}, u32[]{:S(2)}, u32[]{:S(2)}) %all-to-all-start.2) | async-done | bytes 4194336 | tf_op jit(solution)/shard_map/all_to_all | solution.py:134
  175.3 5.7 %reshape.122 = bf16[32,65536]{1,0:T(8,128)(2,1)} reshape(bf16[16,64,2048]{2,1,0:T(8,128)(2,1)} %all-to-all-done.2) | data formatting | bytes 8388608 | tf_op jit(solution)/shard_map/reshape | solution.py:139
  181.0 5.0 %fusion.24 = f32[16,65536]{1,0:T(8,128)} fusion(bf16[32,65536]{1,0:T(8,128)(2,1)} %reshape.122, s32[16]{0:T(128)S(1)} %multiply_add_fusion), kind=kOutput, calls=%fused_computation.39 | convolution fusion | flops 67109376 | bytes 8388672 | tf_op jit(solution)/shard_map/dot_general | solution.py:137
  186.0 4.0 %reshape.123 = f32[512,2048]{1,0:T(8,128)} reshape(f32[16,65536]{1,0:T(8,128)} %fusion.24) | data formatting | bytes 8388608 | tf_op jit(solution)/shard_map/reshape | solution.py:142
  189.9 27.0 %all-gather.6.cloned.1.call-done = bf16[2048,2048]{1,0:T(8,128)(2,1)} async-done(((bf16[16,2048]{1,0:T(8,128)(2,1)}), bf16[2048,2048]{1,0:T(8,128)(2,1)}) %all-gather.6.cloned.1.call-update) | async-done | bytes 8388624 | tf_op jit(solution)/shard_map/all_gather | solution.py:89
  216.9 8.7 %convolution_add_fusion = f32[512,2048]{1,0:T(8,128)S(1)} fusion(f32[512,2048]{1,0:T(8,128)} %reshape.123, bf16[512,2048]{1,0:T(8,128)(2,1)S(1)} %copy-done.3, bf16[2048,2048]{1,0:T(8,128)(2,1)} %all-gather.6.cloned.1.call-done), kind=kOutput, calls=%fused_computation.26 | convolution fusion | flops 4296015872 | bytes 18874368 | tf_op jit(solution)/shard_map/dot_general | solution.py:87
  225.6 4.3 %bitcast_bitcast_fusion = bf16[16,512,128]{2,1,0:T(8,128)(2,1)} fusion(f32[512,2048]{1,0:T(8,128)S(1)} %convolution_add_fusion, f32[510,2048]{1,0:T(8,128)S(1)} %bitcast.75, pred[512]{0:T(512)(128)(4,1)S(1)} %concatenate.14, f32[2048]{0:T(1024)S(1)} %bitcast.81, f32[511,2048]{1,0:T(8,128)S(1)} %bitcast.76, pred[512]{0:T(512)(128)(4,1)S(1)} %pad_add_fusion, ...), kind=kLoop, calls=%fused_computation.27 | loop fusion | flops 13631488 | bytes 14681088 | tf_op jit(solution)/shard_map/transpose | solution.py:46
  230.0 40.6 %while.13 = (s32[]{:T(128)}, bf16[16,512,128]{1,2,0:T(8,128)(2,1)}, bf16[16,512,16]{1,2,0:T(8,128)(2,1)S(1)}, bf16[16,512,16]{1,2,0:T(8,128)(2,1)S(1)}, bf16[16,...) while((s32[]{:T(128)}, bf16[16,512,128]{1,2,0:T(8,128)(2,1)}, ...), condition=%wide.region_7.8_spmd.clone, body=%wide.region_5.7_spmd.clone.sunk | while | flops 78511616 | bytes 1878093 | solution.py:61
  230.0 0.5 fusion.60
  230.4 1.4 fusion.61
  232.0 0.7 constant_dynamic-update-slice_fusion.2
  233.1 1.3 fusion.61
  234.5 0.7 constant_dynamic-update-slice_fusion.2
  235.7 1.3 fusion.61
  237.0 0.7 constant_dynamic-update-slice_fusion.2
  237.7 0.5 fusion.60
  238.2 1.3 fusion.61
  239.6 0.7 constant_dynamic-update-slice_fusion.2
  240.7 1.3 fusion.61
  242.1 0.7 constant_dynamic-update-slice_fusion.2
  243.2 1.3 fusion.61
  244.6 0.7 constant_dynamic-update-slice_fusion.2
  245.8 1.3 fusion.61
  247.2 0.7 constant_dynamic-update-slice_fusion.2
  248.3 1.3 fusion.61
  249.7 0.7 constant_dynamic-update-slice_fusion.2
  250.8 1.3 fusion.61
  252.2 0.7 constant_dynamic-update-slice_fusion.2
  252.9 0.5 fusion.60
  253.4 1.3 fusion.61
  254.8 0.7 constant_dynamic-update-slice_fusion.2
  255.9 1.3 fusion.61
  257.3 0.7 constant_dynamic-update-slice_fusion.2
  258.0 0.5 fusion.60
  258.4 1.3 fusion.61
  259.8 0.7 constant_dynamic-update-slice_fusion.2
  261.0 1.3 fusion.61
  262.4 0.7 constant_dynamic-update-slice_fusion.2
  263.5 1.3 fusion.61
  264.9 0.7 constant_dynamic-update-slice_fusion.2
  266.0 1.3 fusion.61
  267.4 0.7 constant_dynamic-update-slice_fusion.2
  268.5 1.3 fusion.61
  269.9 0.7 constant_dynamic-update-slice_fusion.2
  270.6 16.7 %all-gather.8.cloned.1.call-done = bf16[2048,2048]{1,0:T(8,128)(2,1)} async-done(((bf16[16,2048]{1,0:T(8,128)(2,1)}), bf16[2048,2048]{1,0:T(8,128)(2,1)}) %all-gather.8.cloned.1.call-update) | async-done | bytes 8388624 | tf_op jit(solution)/shard_map/all_gather | solution.py:151
  287.3 9.9 %fusion.16 = bf16[512,2048]{1,0:T(8,128)(2,1)} fusion(bf16[512,2048]{1,0:T(8,128)(2,1)S(1)} %copy-done.2, bf16[512,2048]{0,1:T(8,128)(2,1)} %bitcast.85, bf16[2048,2048]{1,0:T(8,128)(2,1)} %all-gather.8.cloned.1.call-done), kind=kOutput, calls=%fused_computation.24 | convolution fusion | flops 4298113024 | bytes 14680064 | tf_op jit(solution)/shard_map/dot_general | solution.py:149
  (64 shorter events, 8.7 us)
Async XLA Ops:
  6.5 98.3 %copy-start = (bf16[4,16,2048]{2,1,0:T(8,128)(2,1)S(1)}, bf16[4,16,2048]{2,1,0:T(8,128)(2,1)}, u32[]{:S(2)}) copy-start(bf16[4,16,2048]{2,1,0:T(8,128)(2,1)} %param.19) | copy-start | bytes 786436
  6.5 112.4 %all-gather.4.cloned.1.call-start = ((), (), s32[]{:S(2)}) async-start(), calls=%async_computation.3 | async-start | bytes 2113536 | tf_op jit(solution)/shard_map/all_gather | solution.py:84
  7.3 209.6 %all-gather.6.cloned.1.call-start = ((), (), s32[]{:S(2)}) async-start(), calls=%async_computation.4 | async-start | bytes 8454144 | tf_op jit(solution)/shard_map/all_gather | solution.py:89
  11.3 24.2 %all-to-all-start = ((bf16[16,1,64]{2,1,0:T(2,128)(2,1)}), bf16[16,1,64]{2,1,0:T(2,128)(2,1)S(1)}, u32[]{:S(2)}, u32[]{:S(2)}) async-start(bf16[16,1,64]{2,1,0:T(2,128)(2,1)} %convert_element_type.107), calls=%async_computation | async-start | bytes 16384 | tf_op jit(solution)/shard_map/all_to_all | solution.py:125
  35.4 69.4 %copy-start.4 = (bf16[4,16,2048]{2,1,0:T(8,128)(2,1)S(1)}, bf16[4,16,2048]{2,1,0:T(8,128)(2,1)}, u32[]{:S(2)}) copy-start(bf16[4,16,2048]{2,1,0:T(8,128)(2,1)} %param.18) | copy-start | bytes 786436
  35.5 69.4 %all-to-all-start.1 = ((bf16[16,64,2048]{2,1,0:T(8,128)(2,1)}), bf16[16,64,2048]{2,1,0:T(8,128)(2,1)}, u32[]{:S(2)}, u32[]{:S(2)}) async-start(bf16[16,64,2048]{2,1,0:T(8,128)(2,1)} %reshape.119), calls=%async_computation.1 | async-start | bytes 8388608 | tf_op jit(solution)/shard_map/all_to_all | solution.py:124
  42.3 245.0 %all-gather.8.cloned.1.call-start = ((), (), s32[]{:S(2)}) async-start(), calls=%async_computation.5 | async-start | bytes 8454144 | tf_op jit(solution)/shard_map/all_gather | solution.py:151
  113.4 4.9 %copy-start.6 = (s32[1,8]{1,0:T(1,128)S(1)}, s32[1,8]{1,0:T(1,128)}, u32[]{:S(2)}) copy-start(s32[1,8]{1,0:T(1,128)} %param.20) | copy-start | bytes 100
  113.4 5.5 %copy-start.5 = (f32[3,2048]{1,0:T(4,128)S(1)}, f32[3,2048]{1,0:T(4,128)}, u32[]{:S(2)}) copy-start(f32[3,2048]{1,0:T(4,128)} %param.17) | copy-start | bytes 73732
  113.4 5.5 %copy-start.3 = (bf16[512,2048]{1,0:T(8,128)(2,1)S(1)}, bf16[512,2048]{1,0:T(8,128)(2,1)}, u32[]{:S(2)}) copy-start(bf16[512,2048]{1,0:T(8,128)(2,1)} %fusion.15) | copy-start | bytes 6291460
  113.4 62.0 %all-to-all-start.2 = ((bf16[16,64,2048]{2,1,0:T(8,128)(2,1)}), bf16[16,64,2048]{2,1,0:T(8,128)(2,1)}, u32[]{:S(2)}, u32[]{:S(2)}) async-start(bf16[16,64,2048]{2,1,0:T(8,128)(2,1)} %multiply_convert_fusion), calls=%async_computation.2 | async-start | bytes 8388608 | tf_op jit(solution)/shard_map/all_to_all | solution.py:134
  230.0 57.3 %copy-start.2 = (bf16[512,2048]{1,0:T(8,128)(2,1)S(1)}, bf16[512,2048]{1,0:T(8,128)(2,1)}, u32[]{:S(2)}) copy-start(bf16[512,2048]{1,0:T(8,128)(2,1)} %param.12) | copy-start | bytes 6291460
  287.3 9.9 %copy-start.1 = (bf16[4,16,2048]{2,1,0:T(8,128)(2,1)S(1)}, bf16[4,16,2048]{2,1,0:T(8,128)(2,1)}, u32[]{:S(2)}) copy-start(bf16[4,16,2048]{2,1,0:T(8,128)(2,1)} %param.19) | copy-start | bytes 786436
Sparse Core Ops, SparseCore 0:
  10.3 105.3 all-gather.3
  118.9 97.9 all-gather.5
  220.0 67.2 all-gather.7
where the time goes:
time: 305 us; the launch traced here: 304 us
  waiting for transfers between devices  161 us (53%)
  matrix products  66.9 us (22%)
  local copies, waits for them, and re-layouts  31 us (10%)
  starting transfers between devices  19.4 us (6%)
  between operations  13.2 us (4%)
  other arithmetic  12 us (4%)
    all_to_all x1, waiting for transfers between devices, local(): lax.all_to_all(outgoing, 'mp', split_axis=0, concat_axis=0, tiled=True)  61.8 us
    all_to_all x1, waiting for transfers between devices, local(): lax.all_to_all(value_update.astype(jnp.bfloat16), 'mp', split_axis=0, con...  53.5 us
    all_gather x1, waiting for transfers between devices, local(): lax.all_gather(value_weight, ('dp', 'mp'), axis=0, tiled=True)  27 us
    dot_general x16, matrix products, one_head(): jnp.dot(weight.astype(jnp.bfloat16), value_one, preferred_element_type=jn...  20.4 us
    all_gather x1, waiting for transfers between devices, local(): lax.all_gather(output_weight, ('dp', 'mp'), axis=0, tiled=True)  16.7 us
    dynamic_update_slice x32, local copies, waits for them, and re-layouts, taylor_heads(): outputs = lax.map(one_head, (queries, key_rows, value_rows))  12.5 us
    dot_general x1, matrix products, local(): jnp.dot(inputs, lax.all_gather(output_weight, ('dp', 'mp'), axis=0, tiled...  9.94 us
    dot_general x1, matrix products, local(): jnp.dot(inputs, lax.all_gather(value_weight, ('dp', 'mp'), axis=0, tiled=...  8.73 us
  transfers between devices with their start and end apart: 6, of which 4 were waited for; matrix products, arithmetic and copies ran while one was open for 33% of the time, Pallas kernels for 0%

commit v1 on v0

--- a/solution.py
+++ b/solution.py
@@ -86,7 +86,12 @@
     )
     plain_value_rows = jnp.dot(
         inputs,
-        lax.all_gather(value_weight, ("dp", "mp"), axis=0, tiled=True),
+        jnp.concatenate(
+            lax.all_to_all(
+                jnp.stack([value_weight] * lax.axis_size(("dp", "mp"))), ("dp", "mp"), 0, 0
+            ),
+            axis=0,
+        ),
         preferred_element_type=jnp.float32,
     )
     query_key = qk_sum.astype(jnp.bfloat16)

time: 305 us -> 365 us (1.20)
  waiting for transfers between devices: 161 us -> 203 us
  starting transfers between devices: 19.4 us -> 31 us
  local copies, waits for them, and re-layouts: 31 us -> 35.2 us
    all_gather x1, waiting for transfers between devices: 0.02 us -> 77 us  [local(): lax.all_gather(query_key_weight, ('dp', 'mp'), axis=0, tiled=True)]
    all_gather x1 -> x0, waiting for transfers between devices: 27 us -> none  [local(): lax.all_gather(value_weight, ('dp', 'mp'), axis=0, tiled=True)]
    all_gather x1, waiting for transfers between devices: 16.7 us -> 2.73 us  [local(): lax.all_gather(output_weight, ('dp', 'mp'), axis=0, tiled=True)]
    all_to_all x0 -> x1, starting transfers between devices: none -> 11.5 us  [local(): lax.all_to_all(jnp.stack([value_weight] * lax.axis_size(('dp', 'mp'))), (...]
    another operation x0 -> x1, local copies, waits for them, and re-layouts: none -> 4.29 us  [local(): jnp.stack([value_weight] * lax.axis_size(('dp', 'mp')))]
    all_to_all x0 -> x1, waiting for transfers between devices: none -> 4.04 us  [local(): lax.all_to_all(jnp.stack([value_weight] * lax.axis_size(('dp', 'mp'))), (...]
  transfers between devices with their start and end apart: 6 -> 6, of which waited for: 4 -> 5; matrix products, arithmetic and copies ran while one was open for 33% -> 26% of each run, Pallas kernels for 0% -> 0%
where the time goes in v1:
time: 365 us; the launch traced here: 362 us
  waiting for transfers between devices  203 us (56%)
  matrix products  67.1 us (18%)
  local copies, waits for them, and re-layouts  35.2 us (10%)
  starting transfers between devices  31 us (8%)
  between operations  13.5 us (4%)
  other arithmetic  12.1 us (3%)
    all_gather x1, waiting for transfers between devices, local(): lax.all_gather(query_key_weight, ('dp', 'mp'), axis=0, tiled=True)  77 us
    all_to_all x1, waiting for transfers between devices, local(): lax.all_to_all(outgoing, 'mp', split_axis=0, concat_axis=0, tiled=True)  60.9 us
    all_to_all x1, waiting for transfers between devices, local(): lax.all_to_all(value_update.astype(jnp.bfloat16), 'mp', split_axis=0, con...  56.9 us
    dot_general x16, matrix products, one_head(): jnp.dot(weight.astype(jnp.bfloat16), value_one, preferred_element_type=jn...  20.6 us
    dynamic_update_slice x32, local copies, waits for them, and re-layouts, taylor_heads(): outputs = lax.map(one_head, (queries, key_rows, value_rows))  12.4 us
    all_to_all x1, starting transfers between devices, local(): lax.all_to_all(jnp.stack([value_weight] * lax.axis_size(('dp', 'mp'))), (...  11.5 us
    dot_general x1, matrix products, local(): jnp.dot(inputs, lax.all_gather(output_weight, ('dp', 'mp'), axis=0, tiled...  9.94 us
    dot_general x1, matrix products, local(): jnp.dot(inputs, jnp.concatenate(lax.all_to_all(jnp.stack([value_weight] *...  8.76 us
  transfers between devices with their start and end apart: 6, of which 5 were waited for; matrix products, arithmetic and copies ran while one was open for 26% of the time, Pallas kernels for 0%

profile of v1, /device:TPU:1, one launch (start us, length us, event | category | flops | bytes accessed | tf_op | source)
XLA Modules:
  0.0 361.8 jit_solution(9743019757618046526)
XLA Ops:
  6.5 0.7 and_select_fusion.2
  7.5 0.7 multiply_add_fusion
  8.2 0.8 fusion.19
  9.2 0.7 convert_element_type.107
  9.9 7.6 %all-to-all-start.1 = ((bf16[16,1,64]{2,1,0:T(2,128)(2,1)}), bf16[16,1,64]{2,1,0:T(2,128)(2,1)S(1)}, u32[]{:S(2)}, u32[]{:S(2)}) async-start(bf16[16,1,64]{2,1,0:T(2,128)(2,1)} %convert_element_type.107), calls=%async_computation.1 | async-start | bytes 16384 | tf_op jit(solution)/shard_map/all_to_all | solution.py:130
  17.4 2.1 fusion.13
  19.5 3.5 fusion.15
  23.0 2.2 reshape.124
  25.2 3.2 convolution_convert_fusion
  28.4 5.6 %reshape.125 = bf16[16,64,2048]{2,1,0:T(8,128)(2,1)} reshape(bf16[32,65536]{1,0:T(8,128)(2,1)} %convolution_convert_fusion) | data formatting | bytes 8388608 | tf_op jit(solution)/shard_map/reshape | solution.py:117
  34.1 6.8 %all-to-all-start.2 = ((bf16[16,64,2048]{2,1,0:T(8,128)(2,1)}), bf16[16,64,2048]{2,1,0:T(8,128)(2,1)}, u32[]{:S(2)}, u32[]{:S(2)}) async-start(bf16[16,64,2048]{2,1,0:T(8,128)(2,1)} %reshape.125), calls=%async_computation.2 | async-start | bytes 8388608 | tf_op jit(solution)/shard_map/all_to_all | solution.py:129
  40.9 60.9 %all-to-all-done.2 = bf16[16,64,2048]{2,1,0:T(8,128)(2,1)} async-done(((bf16[16,64,2048]{2,1,0:T(8,128)(2,1)}), bf16[16,64,2048]{2,1,0:T(8,128)(2,1)}, u32[]{:S(2)}, u32[]{:S(2)}) %all-to-all-start.2) | async-done | bytes 4194336 | tf_op jit(solution)/shard_map/all_to_all | solution.py:129
  101.8 8.5 %multiply_convert_fusion = bf16[16,64,2048]{2,1,0:T(8,128)(2,1)} fusion(bf16[64,2048,1]{1,0,2:T(8,128)(2,1)S(1)} %bitcast.75, bf16[16,64,2048]{2,1,0:T(8,128)(2,1)} %all-to-all-done.2, bf16[64,2048,1]{1,0,2:T(8,128)(2,1)S(1)} %bitcast.80, f32[64]{0:T(128)S(1)} %fusion.29, f32[16,64]{1,0:T(8,128)S(1)} %bitcast.84), kind=kOutput, calls=%fused_computation.17 | convolution fusion | flops 541261824 | bytes 8917248 | tf_op jit(solution)/shard_map/skc,cd->skd/dot_general | solution.py:136
  110.3 4.9 %all-to-all-start.3 = ((bf16[16,64,2048]{2,1,0:T(8,128)(2,1)}), bf16[16,64,2048]{2,1,0:T(8,128)(2,1)}, u32[]{:S(2)}, u32[]{:S(2)}) async-start(bf16[16,64,2048]{2,1,0:T(8,128)(2,1)} %multiply_convert_fusion), calls=%async_computation.3 | async-start | bytes 8388608 | tf_op jit(solution)/shard_map/all_to_all | solution.py:139
  115.2 0.7 all-gather.3.cloned.1.call-update
  115.9 56.9 %all-to-all-done.3 = bf16[16,64,2048]{2,1,0:T(8,128)(2,1)} async-done(((bf16[16,64,2048]{2,1,0:T(8,128)(2,1)}), bf16[16,64,2048]{2,1,0:T(8,128)(2,1)}, u32[]{:S(2)}, u32[]{:S(2)}) %all-to-all-start.3) | async-done | bytes 4194336 | tf_op jit(solution)/shard_map/all_to_all | solution.py:139
  172.7 4.3 %stack.2 = bf16[128,16,2048]{2,1,0:T(8,128)(2,1)} broadcast(bf16[16,2048]{1,0:T(8,128)(2,1)S(1)} %copy-done.5), dimensions={1,2} | broadcast | bytes 8454144 | tf_op jit(solution)/shard_map/stack | solution.py:91
  177.0 11.5 %all-to-all-start = ((bf16[128,16,2048]{2,1,0:T(8,128)(2,1)}), bf16[128,16,2048]{2,1,0:T(8,128)(2,1)}, u32[]{:S(2)}, u32[]{:S(2)}) async-start(bf16[128,16,2048]{2,1,0:T(8,128)(2,1)} %stack.2), calls=%async_computation | async-start | bytes 16777216 | tf_op jit(solution)/shard_map/all_to_all | solution.py:90
  188.7 0.5 all-gather.5.cloned.1.call-update
  189.9 77.0 %all-gather.3.cloned.1.call-done = bf16[2048,512]{1,0:T(8,128)(2,1)} async-done(((bf16[16,512]{1,0:T(8,128)(2,1)}), bf16[2048,512]{1,0:T(8,128)(2,1)}) %all-gather.3.cloned.1.call-update) | async-done | bytes 2097168 | tf_op jit(solution)/shard_map/all_gather | solution.py:84
  266.9 2.9 convolution_convert_fusion.1
  269.8 5.6 %reshape.128 = bf16[32,65536]{1,0:T(8,128)(2,1)} reshape(bf16[16,64,2048]{2,1,0:T(8,128)(2,1)} %all-to-all-done.3) | data formatting | bytes 8388608 | tf_op jit(solution)/shard_map/reshape | solution.py:144
  275.4 5.0 %fusion.24 = f32[16,65536]{1,0:T(8,128)} fusion(bf16[32,65536]{1,0:T(8,128)(2,1)} %reshape.128, s32[16]{0:T(128)S(1)} %multiply_add_fusion), kind=kOutput, calls=%fused_computation.39 | convolution fusion | flops 67109376 | bytes 8388672 | tf_op jit(solution)/shard_map/dot_general | solution.py:142
  280.4 4.0 %reshape.129 = f32[512,2048]{1,0:T(8,128)} reshape(f32[16,65536]{1,0:T(8,128)} %fusion.24) | data formatting | bytes 8388608 | tf_op jit(solution)/shard_map/reshape | solution.py:147
  284.4 4.0 %all-to-all-done = bf16[128,16,2048]{2,1,0:T(8,128)(2,1)} async-done(((bf16[128,16,2048]{2,1,0:T(8,128)(2,1)}), bf16[128,16,2048]{2,1,0:T(8,128)(2,1)}, u32[]{:S(2)}, u32[]{:S(2)}) %all-to-all-start) | async-done | bytes 8388640 | tf_op jit(solution)/shard_map/all_to_all | solution.py:90
  288.5 8.8 %convolution_add_fusion = f32[512,2048]{1,0:T(8,128)S(1)} fusion(f32[512,2048]{1,0:T(8,128)} %reshape.129, bf16[512,2048]{1,0:T(8,128)(2,1)S(1)} %copy-done.3, bf16[2048,2048]{1,0:T(8,128)(2,1)} %bitcast.5), kind=kOutput, calls=%fused_computation.26 | convolution fusion | flops 4296015872 | bytes 18874368 | tf_op jit(solution)/shard_map/dot_general | solution.py:87
  297.2 4.3 %bitcast_bitcast_fusion = bf16[16,512,128]{2,1,0:T(8,128)(2,1)} fusion(f32[512,2048]{1,0:T(8,128)S(1)} %convolution_add_fusion, f32[510,2048]{1,0:T(8,128)S(1)} %bitcast.76, pred[512]{0:T(512)(128)(4,1)S(1)} %concatenate.14, f32[2048]{0:T(1024)S(1)} %bitcast.82, f32[511,2048]{1,0:T(8,128)S(1)} %bitcast.77, pred[512]{0:T(512)(128)(4,1)S(1)} %pad_add_fusion, ...), kind=kLoop, calls=%fused_computation.27 | loop fusion | flops 13631488 | bytes 14681088 | tf_op jit(solution)/shard_map/transpose | solution.py:46
  301.6 40.7 %while.13 = (s32[]{:T(128)}, bf16[16,512,128]{1,2,0:T(8,128)(2,1)}, bf16[16,512,16]{1,2,0:T(8,128)(2,1)S(1)}, bf16[16,512,16]{1,2,0:T(8,128)(2,1)S(1)}, bf16[16,...) while((s32[]{:T(128)}, bf16[16,512,128]{1,2,0:T(8,128)(2,1)}, ...), condition=%wide.region_7.8_spmd.clone, body=%wide.region_5.7_spmd.clone.sunk | while | flops 78511616 | bytes 1878093 | solution.py:61
  302.0 1.4 fusion.61
  303.6 0.7 constant_dynamic-update-slice_fusion.2
  304.7 1.3 fusion.61
  306.1 0.7 constant_dynamic-update-slice_fusion.2
  307.2 1.3 fusion.61
  308.6 0.7 constant_dynamic-update-slice_fusion.2
  309.8 1.3 fusion.61
  311.2 0.7 constant_dynamic-update-slice_fusion.2
  311.8 0.5 fusion.60
  312.3 1.3 fusion.61
  313.7 0.7 constant_dynamic-update-slice_fusion.2
  314.8 1.3 fusion.61
  316.2 0.7 constant_dynamic-update-slice_fusion.2
  316.9 0.5 fusion.60
  317.4 1.3 fusion.61
  318.7 0.7 constant_dynamic-update-slice_fusion.2
  319.9 1.3 fusion.61
  321.3 0.7 constant_dynamic-update-slice_fusion.2
  322.4 1.3 fusion.61
  323.8 0.7 constant_dynamic-update-slice_fusion.2
  324.9 1.3 fusion.61
  326.4 0.7 constant_dynamic-update-slice_fusion.2
  327.5 1.3 fusion.61
  328.9 0.7 constant_dynamic-update-slice_fusion.2
  330.1 1.3 fusion.61
  331.5 0.7 constant_dynamic-update-slice_fusion.2
  332.6 1.3 fusion.61
  334.0 0.7 constant_dynamic-update-slice_fusion.2
  335.2 1.3 fusion.61
  336.6 0.7 constant_dynamic-update-slice_fusion.2
  337.7 1.3 fusion.61
  339.1 0.7 constant_dynamic-update-slice_fusion.2
  340.2 1.3 fusion.61
  341.6 0.7 constant_dynamic-update-slice_fusion.2
  342.3 2.7 all-gather.5.cloned.1.call-done
  345.0 9.9 %fusion.16 = bf16[512,2048]{1,0:T(8,128)(2,1)} fusion(bf16[512,2048]{1,0:T(8,128)(2,1)S(1)} %copy-done.2, bf16[512,2048]{0,1:T(8,128)(2,1)} %bitcast.86, bf16[2048,2048]{1,0:T(8,128)(2,1)} %all-gather.5.cloned.1.call-done), kind=kOutput, calls=%fused_computation.24 | convolution fusion | flops 4298113024 | bytes 14680064 | tf_op jit(solution)/shard_map/dot_general | solution.py:154
  (66 shorter events, 9.8 us)
Async XLA Ops:
  6.5 95.3 %copy-start = (bf16[4,16,2048]{2,1,0:T(8,128)(2,1)S(1)}, bf16[4,16,2048]{2,1,0:T(8,128)(2,1)}, u32[]{:S(2)}) copy-start(bf16[4,16,2048]{2,1,0:T(8,128)(2,1)} %param.19) | copy-start | bytes 786436
  9.9 24.2 %all-to-all-start.1 = ((bf16[16,1,64]{2,1,0:T(2,128)(2,1)}), bf16[16,1,64]{2,1,0:T(2,128)(2,1)S(1)}, u32[]{:S(2)}, u32[]{:S(2)}) async-start(bf16[16,1,64]{2,1,0:T(2,128)(2,1)} %convert_element_type.107), calls=%async_computation.1 | async-start | bytes 16384 | tf_op jit(solution)/shard_map/all_to_all | solution.py:130
  34.0 67.8 %copy-start.4 = (bf16[4,16,2048]{2,1,0:T(8,128)(2,1)S(1)}, bf16[4,16,2048]{2,1,0:T(8,128)(2,1)}, u32[]{:S(2)}) copy-start(bf16[4,16,2048]{2,1,0:T(8,128)(2,1)} %param.18) | copy-start | bytes 786436
  34.1 67.7 %all-to-all-start.2 = ((bf16[16,64,2048]{2,1,0:T(8,128)(2,1)}), bf16[16,64,2048]{2,1,0:T(8,128)(2,1)}, u32[]{:S(2)}, u32[]{:S(2)}) async-start(bf16[16,64,2048]{2,1,0:T(8,128)(2,1)} %reshape.125), calls=%async_computation.2 | async-start | bytes 8388608 | tf_op jit(solution)/shard_map/all_to_all | solution.py:129
  110.3 62.5 %copy-start.5 = (bf16[16,2048]{1,0:T(8,128)(2,1)S(1)}, bf16[16,2048]{1,0:T(8,128)(2,1)}, u32[]{:S(2)}) copy-start(bf16[16,2048]{1,0:T(8,128)(2,1)} %param.15) | copy-start | bytes 196612
  110.3 62.5 %all-to-all-start.3 = ((bf16[16,64,2048]{2,1,0:T(8,128)(2,1)}), bf16[16,64,2048]{2,1,0:T(8,128)(2,1)}, u32[]{:S(2)}, u32[]{:S(2)}) async-start(bf16[16,64,2048]{2,1,0:T(8,128)(2,1)} %multiply_convert_fusion), calls=%async_computation.3 | async-start | bytes 8388608 | tf_op jit(solution)/shard_map/all_to_all | solution.py:139
  115.1 151.7 %all-gather.3.cloned.1.call-start = ((), (), s32[]{:S(2)}) async-start(), calls=%async_computation.4 | async-start | bytes 2113536 | tf_op jit(solution)/shard_map/all_gather | solution.py:84
  177.0 12.2 %copy-start.7 = (s32[1,8]{1,0:T(1,128)S(1)}, s32[1,8]{1,0:T(1,128)}, u32[]{:S(2)}) copy-start(s32[1,8]{1,0:T(1,128)} %param.20) | copy-start | bytes 100
  177.0 12.8 %copy-start.6 = (f32[3,2048]{1,0:T(4,128)S(1)}, f32[3,2048]{1,0:T(4,128)}, u32[]{:S(2)}) copy-start(f32[3,2048]{1,0:T(4,128)} %param.17) | copy-start | bytes 73732
  177.0 89.8 %copy-start.3 = (bf16[512,2048]{1,0:T(8,128)(2,1)S(1)}, bf16[512,2048]{1,0:T(8,128)(2,1)}, u32[]{:S(2)}) copy-start(bf16[512,2048]{1,0:T(8,128)(2,1)} %fusion.15) | copy-start | bytes 6291460
  177.0 111.4 %all-to-all-start = ((bf16[128,16,2048]{2,1,0:T(8,128)(2,1)}), bf16[128,16,2048]{2,1,0:T(8,128)(2,1)}, u32[]{:S(2)}, u32[]{:S(2)}) async-start(bf16[128,16,2048]{2,1,0:T(8,128)(2,1)} %stack.2), calls=%async_computation | async-start | bytes 16777216 | tf_op jit(solution)/shard_map/all_to_all | solution.py:90
  188.5 156.5 %all-gather.5.cloned.1.call-start = ((), (), s32[]{:S(2)}) async-start(), calls=%async_computation.5 | async-start | bytes 8454144 | tf_op jit(solution)/shard_map/all_gather | solution.py:156
  301.6 43.5 %copy-start.2 = (bf16[512,2048]{1,0:T(8,128)(2,1)S(1)}, bf16[512,2048]{1,0:T(8,128)(2,1)}, u32[]{:S(2)}) copy-start(bf16[512,2048]{1,0:T(8,128)(2,1)} %param.12) | copy-start | bytes 6291460
  345.0 9.9 %copy-start.1 = (bf16[4,16,2048]{2,1,0:T(8,128)(2,1)S(1)}, bf16[4,16,2048]{2,1,0:T(8,128)(2,1)}, u32[]{:S(2)}) copy-start(bf16[4,16,2048]{2,1,0:T(8,128)(2,1)} %param.19) | copy-start | bytes 786436
Sparse Core Ops, SparseCore 0:
  118.9 147.8 all-gather.2
  270.0 74.9 all-gather.4
